TPU v7x, 32 devices: a whole 2x2x4 slice. The times are simulated.
32 devices in a mesh: groups: 2 (over y), row: 4 (over z), col: 4 (over x, core).
Axes of the slice: x: 2, y: 2, z: 4, core: 2. Of those that a mesh axis runs over, the one named last changes fastest.
Arguments:
- queries: bfloat16 [4096, 1024], P(('groups', 'row'), 'col'), parts along dimension 0, may hold values from -64 to 64
- keys: bfloat16 [4096, 1024], P(('groups', 'col'), 'row'), parts along dimension 0, may hold values from -6 to 6
- values: bfloat16 [4096, 1024], P(('groups', 'col'), 'row'), parts along dimension 0, may hold values from -6 to 6
- cotangent: bfloat16 [4096, 1024], P(('groups', 'row'), 'col'), parts along dimension 0, may hold values from -6 to 6
- block_lists: int32 [32, 16], P(('groups', 'row')), parts along dimension 0, may hold values from 0 to 15, as said below
- block_counts: int32 [32], P(('groups', 'row')), parts along dimension 0, may hold values from 1 to 16, as said below
Outputs:
- attended: bfloat16 [4096, 1024], P(('groups', 'row'), 'col'), parts along dimension 0
- grad_queries: bfloat16 [4096, 1024], P(('groups', 'row'), 'col'), parts along dimension 0
- grad_keys: bfloat16 [4096, 1024], P(('groups', 'col'), 'row'), parts along dimension 0
- grad_values: bfloat16 [4096, 1024], P(('groups', 'col'), 'row'), parts along dimension 0
There are 2 independent parts, one for each index of `groups`. A program takes and returns all parts, laid end to end along the dimension named above; each array names one. Nothing has to cross between parts.
Inputs may be any that keep to these rules, and one draw needn't show every extreme that they name: `block_lists`: each row lists 16 distinct blocks; its first entry is the query block itself. `block_counts`: some query block has all 16 entries live in every draw.
All inputs are finite; a program needn't handle non-finite values.
Results may differ from a plain program's by a relative error of at most 0.011.
Values may be sent and summed in bfloat16 or wider, within the bound.
No kernel may reach another device: no remote copies, remote signals or barrier semaphores. Data moves between devices by JAX's collectives and lax.ppermute only.
A program may use at most 64 MiB of HBM per device.

v0:
```python
import functools
import math

import jax
import jax.numpy as jnp
from jax import lax
from jax.experimental import pallas as pl
from jax.experimental.pallas import tpu as pltpu
from jax.sharding import PartitionSpec as P

D = 1024
HEADS = 16
HEAD = 64
BLK = 128
MAXNB = 16


NEG_FILL = -1e30
GROUP = 2
STREAMS = 8
TAIL = 16
BATCHES = (1, 2, 1)
HOPS = (2, 3)
VMEM_LIMIT = 40 * 1024 * 1024
VMEM = pl.BlockSpec(memory_space=pltpu.VMEM)
SMEM = pl.BlockSpec(memory_space=pltpu.SMEM)


def pack_body(lists, counts, q_ref, g_ref, k_ref, v_ref, *outs):
    chunks = q_ref.shape[1] // HEAD
    rows = q_ref.shape[0]

    def pack(left_ref, right_ref, out_refs, at):
        for step in range(chunks):
            head = (at + step) % chunks
            lanes = slice(head * HEAD, (head + 1) * HEAD)
            out_refs[step][:rows, :] = jnp.concatenate(
                [left_ref[:, lanes], right_ref[:, lanes]], axis=1
            )

    for at in range(chunks):

        @pl.when(lax.axis_index("col") == at)
        def _():
            pack(k_ref, v_ref, outs[chunks:], at)

        @pl.when(lax.axis_index("row") == at)
        def _():
            pack(q_ref, g_ref, outs[:chunks], at)

    row = lax.broadcasted_iota(jnp.int32, (TAIL, 2 * HEAD), 0)
    lane = lax.broadcasted_iota(jnp.int32, (TAIL, 2 * HEAD), 1)
    table = jnp.zeros((TAIL, 2 * HEAD), jnp.int32)
    for qb in range(rows // BLK):
        line = jnp.where(lane == MAXNB, counts[qb], 0)
        for at in range(MAXNB):
            line = jnp.where(lane == at, lists[qb, at], line)
        table = jnp.where(row == qb, line, table)
    table = table.astype(jnp.float32).astype(jnp.bfloat16)
    for out_ref in outs[:chunks]:
        out_ref[rows:, :] = table


def unpack_body(axis, *refs):
    left_ref, right_ref = refs[-2:]
    chunks = len(refs) - 2
    for at in range(chunks):

        @pl.when(lax.axis_index(axis) == at)
        def _():
            parts = [refs[(head - at) % chunks][...] for head in range(chunks)]
            left_ref[...] = jnp.concatenate([p[:, :HEAD] for p in parts], axis=1)
            right_ref[...] = jnp.concatenate([p[:, HEAD:] for p in parts], axis=1)


def fold(x, op):
    return op(x.reshape(x.shape[0] // 8, 8, x.shape[1]), axis=0)


def attend_body(chunks, parts, first, last, *refs):
    def take(count):
        nonlocal refs
        head, refs = refs[:count], refs[count:]
        return head

    x_refs = take(chunks)
    if first:
        kv_refs = take(parts)
    else:
        kv_all, kv_t, acc_in = take(3)
    og_refs = take(chunks)
    gkv_refs = take(parts) if last else ()
    acc_out = () if last else take(1)
    if first:
        kv_all, kv_t = take(2)
    wide, table, items, both, both_t, stat, tiles, tops, sem, table_sem = take(10)
    (outs,) = take(1)
    stats = take(STREAMS)
    acc = take(1)[0] if last else acc_out[0]
    scale = 1.0 / math.sqrt(HEAD)
    to_log2 = scale * math.log2(math.e)
    rows = kv_all.shape[0] // parts
    per_chunk = rows // BLK
    blocks = chunks * per_chunk

    lane = lax.broadcasted_iota(jnp.int32, (TAIL, 2 * HEAD), 1)
    for c in range(chunks):
        listed = x_refs[c][rows:, :].astype(jnp.float32).astype(jnp.int32)
        part = lax.rem(lax.axis_index("col") - lax.div(listed, per_chunk) + parts, parts)
        slot = part * per_chunk + lax.rem(listed, per_chunk)
        wide[c * TAIL : (c + 1) * TAIL, :] = jnp.where(lane < MAXNB, slot, listed)
    table_copy = pltpu.make_async_copy(wide, table, table_sem)
    table_copy.start()

    copies = []
    if first:
        for c in range(parts):
            copies.append(
                pltpu.make_async_copy(
                    kv_refs[c], kv_all.at[pl.ds(c * rows, rows), :], sem.at[c]
                )
            )
    for copy in copies:
        copy.start()
    if first:
        acc[...] = jnp.zeros_like(acc)
    else:
        acc[...] = acc_in[...]
    outs[...] = jnp.zeros_like(outs)
    for s in range(STREAMS):
        stats[s][0] = jnp.full(stats[s].shape[1:], NEG_FILL, jnp.float32)
        stats[s][1] = jnp.zeros(stats[s].shape[1:], jnp.float32)
        stats[s][2] = jnp.zeros(stats[s].shape[1:], jnp.float32)

    is_left = lax.broadcasted_iota(jnp.int32, (BLK, 2 * HEAD), 1) < HEAD
    zeros = jnp.zeros((HEAD, BLK), jnp.bfloat16)
    for b in range(blocks):
        at = (b % per_chunk) * BLK
        x = x_refs[b // per_chunk][at : at + BLK, :]
        both[b, :BLK, :] = jnp.where(is_left, x, jnp.zeros_like(x))
        both[b, BLK:, :] = jnp.where(is_left, jnp.zeros_like(x), x)
        x_t = x.T
        both_t[b, :HEAD, :BLK] = x_t[:HEAD]
        both_t[b, :HEAD, BLK:] = zeros
        both_t[b, HEAD:, :BLK] = zeros
        both_t[b, HEAD:, BLK:] = x_t[HEAD:]
    if first:
        for c in range(parts):
            for b in range(per_chunk):
                at = c * rows + b * BLK
                kv_t[:, at : at + BLK] = kv_refs[c][b * BLK : (b + 1) * BLK, :].T
    for copy in copies:
        copy.wait()
    table_copy.wait()

    def line(qb):
        return lax.div(qb, per_chunk) * TAIL + lax.rem(qb, per_chunk)

    def add_items(qb, count):
        groups = (table[line(qb), MAXNB] + GROUP - 1) // GROUP

        def add_item(g, _):
            items[0, count + g] = qb
            items[1, count + g] = g * GROUP
            return 0

        lax.fori_loop(0, groups, add_item, 0)
        return count + groups

    count = lax.fori_loop(0, blocks, add_items, 0)
    steps = (count + STREAMS - 1) // STREAMS
    for s in range(STREAMS - 1):
        items[0, count + s] = 0
        items[1, count + s] = MAXNB

    def item(at):
        qb, base = items[0, at], items[1, at]
        slots = [
            pl.multiple_of(table[line(qb), jnp.minimum(base + u, MAXNB - 1)] * BLK, BLK)
            for u in range(GROUP)
        ]
        return qb, base, slots

    def score_step(i, _):
        for s in range(STREAMS):
            at = s * steps + i
            qb, base, slots = item(at)
            live = table[line(qb), MAXNB]
            kv = jnp.concatenate([kv_all[pl.ds(k, BLK), :] for k in slots], axis=0)
            both_scores = jnp.dot(kv, both_t[qb], preferred_element_type=jnp.float32)
            scores = [
                both_scores[u * BLK : (u + 1) * BLK, :BLK] * to_log2
                + jnp.where(base + u < live, 0.0, NEG_FILL)
                for u in range(GROUP)
            ]
            top = functools.reduce(jnp.maximum, [fold(v, jnp.max) for v in scores])
            top = jnp.max(top, axis=0, keepdims=True)
            total = jnp.zeros((8, BLK), jnp.float32)
            dot = jnp.zeros((8, BLK), jnp.float32)
            for u in range(GROUP):
                part = slice(u * BLK, (u + 1) * BLK)
                e = jnp.exp2(scores[u] - top)
                dw = both_scores[part, BLK:]
                tiles[at, part, :BLK] = e
                tiles[at, part, BLK:] = dw
                total = total + fold(e, jnp.sum)
                dot = dot + fold(e * dw, jnp.sum)
            total = jnp.sum(total, axis=0, keepdims=True)
            dot = jnp.sum(dot, axis=0, keepdims=True)
            tops[pl.ds(at, 1), :] = top
            row = pl.ds(qb, 1)
            old = stats[s][0, row, :]
            new = jnp.maximum(old, top)
            old_part, new_part = jnp.exp2(old - new), jnp.exp2(top - new)
            stats[s][0, row, :] = new
            stats[s][1, row, :] = stats[s][1, row, :] * old_part + total * new_part
            stats[s][2, row, :] = stats[s][2, row, :] * old_part + dot * new_part
        return 0

    lax.fori_loop(0, steps, score_step, 0)

    top = functools.reduce(jnp.maximum, [st[0] for st in stats])
    total = functools.reduce(jnp.add, [st[1] * jnp.exp2(st[0] - top) for st in stats])
    dot = functools.reduce(jnp.add, [st[2] * jnp.exp2(st[0] - top) for st in stats])
    stat[0] = top
    stat[1] = 1.0 / total
    stat[2] = dot / total

    def grad_step(i, _):
        for s in range(STREAMS):
            at = s * steps + i
            qb, base, slots = item(at)
            row = pl.ds(qb, 1)
            factor = stat[1, row, :] * jnp.exp2(tops[pl.ds(at, 1), :] - stat[0, row, :])
            delta = stat[2, row, :]
            w, ds = [], []
            for u in range(GROUP):
                part = slice(u * BLK, (u + 1) * BLK)
                weights = tiles[at, part, :BLK] * factor
                ds.append((weights * (tiles[at, part, BLK:] - delta)).astype(jnp.bfloat16))
                w.append(weights.astype(jnp.bfloat16))
            pair = jnp.concatenate(
                [jnp.concatenate(ds, axis=0), jnp.concatenate(w, axis=0)], axis=1
            )
            grads = jnp.dot(pair, both[qb], preferred_element_type=jnp.float32)
            for u in range(GROUP):
                acc[pl.ds(slots[u], BLK), :] += grads[u * BLK : (u + 1) * BLK]
            t = jnp.concatenate([kv_t[:, pl.ds(k, BLK)] for k in slots], axis=1)
            sums = jnp.dot(t, pair, preferred_element_type=jnp.float32)
            outs[qb, :HEAD, :] += sums[HEAD:, BLK:]
            outs[qb, HEAD:, :] += sums[:HEAD, :BLK]
        return 0

    lax.fori_loop(0, steps, grad_step, 0)

    is_out = lax.broadcasted_iota(jnp.int32, (2 * HEAD, BLK), 0) < HEAD
    for b in range(blocks):
        out = outs[b]
        out = jnp.where(is_out, out, out * scale)
        at = (b % per_chunk) * BLK
        og_refs[b // per_chunk][at : at + BLK, :] = out.T.astype(jnp.bfloat16)
    if last:
        for b in range(parts * per_chunk):
            total = acc[b * BLK : (b + 1) * BLK, :]
            at = (b % per_chunk) * BLK
            gkv_refs[b // per_chunk][at : at + BLK, :] = jnp.where(
                is_left, total * scale, total
            ).astype(jnp.bfloat16)


def in_vmem(x):
    return pltpu.with_memory_space_constraint(x, pltpu.VMEM)


def head_per_device(queries, keys, values, cotangent, block_lists, block_counts):
    chunks = 4
    rows = queries.shape[0]
    chunk = pltpu.VMEM((rows, 2 * HEAD), jnp.bfloat16)
    tailed = pltpu.VMEM((rows + TAIL, 2 * HEAD), jnp.bfloat16)
    packed = pl.pallas_call(
        pack_body,
        out_shape=[tailed] * chunks + [chunk] * chunks,
        in_specs=[SMEM] * 2 + [VMEM] * 4,
        out_specs=[VMEM] * (2 * chunks),
        name="pack",
    )(block_lists, block_counts, queries, cotangent, keys, values)

    def q_perm(step):
        return [
            (r * chunks + c, c * chunks + (r + step) % chunks)
            for r in range(chunks)
            for c in range(chunks)
        ]

    def k_perm(step):
        return [(c, (c + step) % chunks) for c in range(chunks)]

    def swap(perm):
        return [(b, a) for a, b in perm]

    axes = ("row", "col")
    kv = [packed[chunks]] + [
        lax.ppermute(packed[chunks + s], "col", k_perm(s)) for s in range(1, chunks)
    ]
    hop = {s: lax.ppermute(packed[s], "col", [(c, c ^ 2) for c in range(chunks)]) for s in HOPS}
    xs = [
        lax.ppermute(
            hop.get(s, packed[s]), axes, [(a ^ 2, b) if s in hop else (a, b) for a, b in q_perm(s)]
        )
        for s in range(chunks)
    ]

    def attend(xs, carried, first, last):
        count = len(xs)
        blocks = count * rows // BLK
        most = blocks * MAXNB // GROUP + STREAMS
        keys_all = pltpu.VMEM((chunks * rows, 2 * HEAD), jnp.bfloat16)
        keys_t = pltpu.VMEM((2 * HEAD, chunks * rows), jnp.bfloat16)
        sums = pltpu.VMEM((chunks * rows, 2 * HEAD), jnp.float32)
        out_shape = [chunk] * count + ([chunk] * chunks if last else [sums])
        if first:
            out_shape += [keys_all, keys_t]
        return pl.pallas_call(
            functools.partial(attend_body, count, chunks, first, last),
            out_shape=out_shape,
            in_specs=[VMEM] * (count + len(carried)),
            out_specs=[VMEM] * len(out_shape),
            scratch_shapes=[
                pltpu.VMEM((count * TAIL, 2 * HEAD), jnp.int32),
                pltpu.SMEM((count * TAIL, 2 * HEAD), jnp.int32),
                pltpu.SMEM((2, most), jnp.int32),
                pltpu.VMEM((blocks, 2 * BLK, 2 * HEAD), jnp.bfloat16),
                pltpu.VMEM((blocks, 2 * HEAD, 2 * BLK), jnp.bfloat16),
                pltpu.VMEM((3, blocks, BLK), jnp.float32),
                pltpu.VMEM((most, GROUP * BLK, 2 * BLK), jnp.float32),
                pltpu.VMEM((most, BLK), jnp.float32),
                pltpu.SemaphoreType.DMA((chunks,)),
                pltpu.SemaphoreType.DMA,
            ]
            + [pltpu.VMEM((blocks, 2 * HEAD, BLK), jnp.float32)]
            + [pltpu.VMEM((3, blocks, BLK), jnp.float32)] * STREAMS
            + ([sums] if last else []),
            compiler_params=pltpu.CompilerParams(vmem_limit_bytes=VMEM_LIMIT),
            name="attend",
        )(*[in_vmem(a) for a in (*xs, *carried)])

    carried = kv
    ogs = []
    for size in BATCHES:
        batch = xs[len(ogs) : len(ogs) + size]
        first, last = not ogs, len(ogs) + size == chunks
        results = attend(batch, carried, first, last)
        ogs += [
            lax.ppermute(results[s], axes, swap(q_perm(len(ogs) + s))) for s in range(size)
        ]
        rest = results[size:]
        if last:
            gkv = rest[:chunks]
        elif first:
            keys_all, keys_t = rest[1:]
        carried = [keys_all, keys_t, rest[0]] if not last else None
    gkv = [gkv[0]] + [lax.ppermute(gkv[s], "col", swap(k_perm(s))) for s in range(1, chunks)]

    whole = jax.ShapeDtypeStruct(queries.shape, jnp.bfloat16)

    def unpack(axis, parts):
        return pl.pallas_call(
            functools.partial(unpack_body, axis),
            out_shape=[whole, whole],
            in_specs=[VMEM] * chunks,
            out_specs=[VMEM, VMEM],
            name="unpack",
        )(*[in_vmem(p) for p in parts])

    attended, grad_queries = unpack("row", ogs)
    grad_keys, grad_values = unpack("col", gkv)
    return attended, grad_queries, grad_keys, grad_values


def tile_scores(query_tile, key_tile, score_scale):
    query_heads = query_tile.reshape(query_tile.shape[0], HEADS, -1)
    key_heads = key_tile.reshape(key_tile.shape[0], HEADS, -1)
    return (
        jnp.einsum("qhd,khd->hqk", query_heads, key_heads, preferred_element_type=jnp.float32)
        * score_scale
    )


def on_device(queries, keys, values, cotangent, block_lists, block_counts):
    score_scale = 1.0 / math.sqrt(HEAD)
    q_full = lax.all_gather(queries, "col", axis=1, tiled=True)
    k_full, v_full = (
        lax.all_gather(keys, "row", axis=1, tiled=True),
        lax.all_gather(values, "row", axis=1, tiled=True),
    )
    q_rows = q_full.shape[0]
    k_rows = k_full.shape[0]
    q_blocks = q_rows // BLK
    k_blocks = k_rows // BLK
    group_size = min(4, q_blocks)
    span_rows = group_size * BLK
    supers = q_blocks // group_size
    tile_count = supers * k_blocks
    first_key = lax.axis_index("col") * k_blocks
    wanted = first_key + jnp.arange(k_blocks, dtype=jnp.int32)
    live_slots = jnp.arange(MAXNB, dtype=jnp.int32)[None, :] < block_counts[:, None]
    block_hit = jnp.any(
        (block_lists[:, :, None] == wanted[None, None, :]) & live_slots[:, :, None], axis=1
    )
    block_hit = block_hit.reshape(supers, group_size, k_blocks).transpose(0, 2, 1)
    row_mask = jnp.repeat(block_hit, BLK, axis=2)
    tile_any = jnp.any(block_hit, axis=2)

    def tile_parts(step):
        super_at = step // k_blocks
        key_at = step % k_blocks
        query_tile = lax.dynamic_slice_in_dim(q_full, super_at * span_rows, span_rows, 0)
        key_tile = lax.dynamic_slice_in_dim(k_full, key_at * BLK, BLK, 0)
        value_tile = lax.dynamic_slice_in_dim(v_full, key_at * BLK, BLK, 0)
        keep_mask = row_mask[super_at, key_at][None, :, None]
        return (super_at, key_at, query_tile, key_tile, value_tile, keep_mask)

    def unchanged(carry):
        return carry

    def stats_step(step, carry):
        super_at, key_at, query_tile, key_tile, value_tile, keep_mask = tile_parts(step)

        def stats_work(state):
            row_top, row_total = state
            scores = jnp.where(keep_mask, tile_scores(query_tile, key_tile, score_scale), NEG_FILL)
            old_top = lax.dynamic_slice_in_dim(row_top, super_at * span_rows, span_rows, 1)
            old_total = lax.dynamic_slice_in_dim(row_total, super_at * span_rows, span_rows, 1)
            new_top = jnp.maximum(old_top, jnp.max(scores, axis=2))
            exp_terms = jnp.where(keep_mask, jnp.exp(scores - new_top[:, :, None]), 0.0)
            fresh = old_total * jnp.exp(old_top - new_top) + jnp.sum(exp_terms, axis=2)
            return (
                lax.dynamic_update_slice_in_dim(row_top, new_top, super_at * span_rows, 1),
                lax.dynamic_update_slice_in_dim(row_total, fresh, super_at * span_rows, 1),
            )

        return lax.cond(tile_any[super_at, key_at], stats_work, unchanged, carry)

    start_top = jnp.full((HEADS, q_rows), NEG_FILL, jnp.float32)
    start_total = jnp.zeros((HEADS, q_rows), jnp.float32)
    local_top, local_total = lax.fori_loop(0, tile_count, stats_step, (start_top, start_total))
    row_top = lax.pmax(local_top.astype(jnp.bfloat16), "col").astype(local_top.dtype)
    row_total = lax.psum(local_total * jnp.exp(local_top - row_top), "col")

    def tile_weights(scores, super_at, keep_mask):
        top_rows = lax.dynamic_slice_in_dim(row_top, super_at * span_rows, span_rows, 1)
        total_rows = lax.dynamic_slice_in_dim(row_total, super_at * span_rows, span_rows, 1)
        ratio = jnp.exp(scores - top_rows[:, :, None]) / total_rows[:, :, None]
        return jnp.where(keep_mask, ratio, 0.0).astype(jnp.bfloat16)

    def output_step(step, carry):
        super_at, key_at, query_tile, key_tile, value_tile, keep_mask = tile_parts(step)

        def output_work(out_rows):
            scores = jnp.where(keep_mask, tile_scores(query_tile, key_tile, score_scale), NEG_FILL)
            weights = tile_weights(scores, super_at, keep_mask)
            value_heads = value_tile.reshape(BLK, HEADS, -1)
            part = jnp.einsum(
                "hqk,khd->qhd", weights, value_heads, preferred_element_type=jnp.float32
            ).reshape(span_rows, -1)
            current = lax.dynamic_slice_in_dim(out_rows, super_at * span_rows, span_rows, 0)
            return lax.dynamic_update_slice_in_dim(
                out_rows, current + part, super_at * span_rows, 0
            )

        return lax.cond(tile_any[super_at, key_at], output_work, unchanged, carry)

    partial_out = lax.fori_loop(0, tile_count, output_step, jnp.zeros((q_rows, D), jnp.float32))
    out_share = lax.psum_scatter(partial_out, "col", scatter_dimension=1, tiled=True).astype(
        jnp.bfloat16
    )
    grad_full, out_full = (
        lax.all_gather(cotangent, "col", axis=1, tiled=True),
        lax.all_gather(out_share, "col", axis=1, tiled=True),
    )
    delta = jnp.einsum(
        "qhd,qhd->hq",
        grad_full.reshape(q_rows, HEADS, -1),
        out_full.reshape(q_rows, HEADS, -1),
        preferred_element_type=jnp.float32,
    )

    def grad_step(step, carry):
        super_at, key_at, query_tile, key_tile, value_tile, keep_mask = tile_parts(step)

        def grad_work(state):
            query_accum, key_accum, value_accum = state
            scores = jnp.where(keep_mask, tile_scores(query_tile, key_tile, score_scale), NEG_FILL)
            weights = tile_weights(scores, super_at, keep_mask)
            grad_tile = lax.dynamic_slice_in_dim(
                grad_full, super_at * span_rows, span_rows, 0
            ).reshape(span_rows, HEADS, -1)
            value_heads = value_tile.reshape(BLK, HEADS, -1)
            key_heads = key_tile.reshape(BLK, HEADS, -1)
            query_heads = query_tile.reshape(span_rows, HEADS, -1)
            dweights = jnp.einsum(
                "qhd,khd->hqk", grad_tile, value_heads, preferred_element_type=jnp.float32
            )
            delta_rows = lax.dynamic_slice_in_dim(delta, super_at * span_rows, span_rows, 1)
            dscores = (weights.astype(jnp.float32) * (dweights - delta_rows[:, :, None])).astype(
                jnp.bfloat16
            )
            query_part = score_scale * jnp.einsum(
                "hqk,khd->qhd", dscores, key_heads, preferred_element_type=jnp.float32
            )
            key_part = score_scale * jnp.einsum(
                "hqk,qhd->khd", dscores, query_heads, preferred_element_type=jnp.float32
            )
            value_part = jnp.einsum(
                "hqk,qhd->khd", weights, grad_tile, preferred_element_type=jnp.float32
            )
            query_now = lax.dynamic_slice_in_dim(query_accum, super_at * span_rows, span_rows, 0)
            key_now = lax.dynamic_slice_in_dim(key_accum, key_at * BLK, BLK, 0)
            value_now = lax.dynamic_slice_in_dim(value_accum, key_at * BLK, BLK, 0)
            query_accum = lax.dynamic_update_slice_in_dim(
                query_accum, query_now + query_part.reshape(span_rows, -1), super_at * span_rows, 0
            )
            key_accum = lax.dynamic_update_slice_in_dim(
                key_accum, key_now + key_part.reshape(BLK, -1), key_at * BLK, 0
            )
            value_accum = lax.dynamic_update_slice_in_dim(
                value_accum, value_now + value_part.reshape(BLK, -1), key_at * BLK, 0
            )
            return (query_accum, key_accum, value_accum)

        return lax.cond(tile_any[super_at, key_at], grad_work, unchanged, carry)

    start_grads = (
        jnp.zeros((q_rows, D), jnp.float32),
        jnp.zeros((k_rows, D), jnp.float32),
        jnp.zeros((k_rows, D), jnp.float32),
    )
    query_parts, key_parts, value_parts = lax.fori_loop(0, tile_count, grad_step, start_grads)
    grad_queries = lax.psum_scatter(query_parts, "col", scatter_dimension=1, tiled=True).astype(
        jnp.bfloat16
    )
    grad_keys, grad_values = (
        lax.psum_scatter(key_parts, "row", scatter_dimension=1, tiled=True),
        lax.psum_scatter(value_parts, "row", scatter_dimension=1, tiled=True),
    )
    return (
        out_share,
        grad_queries,
        grad_keys.astype(jnp.bfloat16),
        grad_values.astype(jnp.bfloat16),
    )


def solution(mesh):
    rows, cols = mesh.shape["row"], mesh.shape["col"]
    one_head = rows == 4 and cols == 4
    return jax.shard_map(
        head_per_device if one_head else on_device,
        mesh=mesh,
        in_specs=(
            P(("groups", "row"), "col"),
            P(("groups", "col"), "row"),
            P(("groups", "col"), "row"),
            P(("groups", "row"), "col"),
            P(("groups", "row"), None),
            P(("groups", "row")),
        ),
        out_specs=(
            P(("groups", "row"), "col"),
            P(("groups", "row"), "col"),
            P(("groups", "col"), "row"),
            P(("groups", "col"), "row"),
        ),
        check_vma=False,
    )
```

profile of v0, /device:TPU:0, one launch (start us, length us, event | category | flops | bytes accessed | tf_op | source)
XLA Modules:
  0.0 58.4 jit_solution(784045043474629358)
XLA Ops:
  0.6 1.7 %pack.1 = (bf16[528,128]{1,0:T(8,128)(2,1)S(1)}, bf16[528,128]{1,0:T(8,128)(2,1)S(1)}, bf16[528,128]{1,0:T(8,128)(2,1)S(1)}, bf16[528,128]{1,0:T(8,128)(2,1)S(1)...) custom-call(s32[4,16]{1,0:T(4,128)} %lists.1, ...), custom_call_target="tpu_custom_call" | custom-call | tf_op jit(solution)/shard_map/pack/pallas_call | solution.py:280
  2.3 3.0 %collective-permute-start.6 = (bf16[528,128]{1,0:T(8,128)(2,1)S(1)}, bf16[528,128]{1,0:T(8,128)(2,1)S(1)}, u32[]{:S(2)}, u32[]{:S(2)}) collective-permute-start(bf16[528,128]{1,0:T(8,128)(2,1)S(1)} %get-tuple-element.35), channel_id=1, source_target_pairs={{0,2},{1,3},{2,0},{3,1},{4,6},{5,7},{6,4},{7,5},{8,10},{9,11},{10,... | collective-permute-start | bytes 405512 | tf_op jit(solution)/shard_map/ppermute | solution.py:305
  5.3 0.0 collective-permute-start.1
  5.3 0.1 collective-permute-start.2
  5.5 1.9 %collective-permute-start.10 = (bf16[528,128]{1,0:T(8,128)(2,1)S(1)}, bf16[528,128]{1,0:T(8,128)(2,1)S(1)}, u32[]{:S(2)}, u32[]{:S(2)}) collective-permute-start(bf16[528,128]{1,0:T(8,128)(2,1)S(1)} %get-tuple-element.41), channel_id=1, source_target_pairs={{0,2},{1,3},{2,0},{3,1},{4,6},{5,7},{6,4},{7,5},{8,10},{9,11},{10,... | collective-permute-start | bytes 405512 | tf_op jit(solution)/shard_map/ppermute | solution.py:305
  7.4 0.7 %collective-permute-start = (bf16[528,128]{1,0:T(8,128)(2,1)S(1)}, bf16[528,128]{1,0:T(8,128)(2,1)S(1)}, u32[]{:S(2)}, u32[]{:S(2)}) collective-permute-start(bf16[528,128]{1,0:T(8,128)(2,1)S(1)} %get-tuple-element.28), channel_id=1, source_target_pairs={{0,0},{1,4},{2,8},{3,12},{4,1},{5,5},{6,9},{7,13},{8,2},{9,6},{10,... | collective-permute-start | bytes 405512 | tf_op jit(solution)/shard_map/ppermute | solution.py:307
  8.0 3.1 %collective-permute-done.1.refs_2_ = bf16[512,128]{1,0:T(8,128)(2,1)S(1)} collective-permute-done((bf16[512,128]{1,0:T(8,128)(2,1)S(1)}, bf16[512,128]{1,0:T(8,128)(2,1)S(1)}, u32[]{:S(2)}, u32[]{:S(2)}) %collective-permute-start.1) | collective-permute-done | bytes 131104 | tf_op jit(solution)/shard_map/ppermute | solution.py:303
  11.2 0.0 collective-permute-start.5
  11.2 0.0 collective-permute-done.6
  11.2 5.1 %collective-permute-start.7 = (bf16[528,128]{1,0:T(8,128)(2,1)S(1)}, bf16[528,128]{1,0:T(8,128)(2,1)S(1)}, u32[]{:S(2)}, u32[]{:S(2)}) collective-permute-start(bf16[528,128]{1,0:T(8,128)(2,1)S(1)} %collective-permute-done.6), channel_id=1, source_target_pairs={{2,2},{3,6},{0,10},{1,14},{6,3},{7,7},{4,11},{5,15},{10,0},{11,4},... | collective-permute-start | bytes 405512 | tf_op jit(solution)/shard_map/ppermute | solution.py:307
  16.2 0.0 collective-permute-done.2.refs_3_
  16.2 0.9 %collective-permute-start.3 = (bf16[512,128]{1,0:T(8,128)(2,1)S(1)}, bf16[512,128]{1,0:T(8,128)(2,1)S(1)}, u32[]{:S(2)}, u32[]{:S(2)}) collective-permute-start(bf16[512,128]{1,0:T(8,128)(2,1)S(1)} %get-tuple-element.32), channel_id=1, source_target_pairs={{0,3},{1,0},{2,1},{3,2},{4,7},{5,4},{6,5},{7,6},{8,11},{9,8},{10,9... | collective-permute-start | bytes 393224 | tf_op jit(solution)/shard_map/ppermute | solution.py:303
  17.1 1.4 %collective-permute-done.10 = bf16[528,128]{1,0:T(8,128)(2,1)S(1)} collective-permute-done((bf16[528,128]{1,0:T(8,128)(2,1)S(1)}, bf16[528,128]{1,0:T(8,128)(2,1)S(1)}, u32[]{:S(2)}, u32[]{:S(2)}) %collective-permute-start.10) | collective-permute-done | bytes 135200 | tf_op jit(solution)/shard_map/ppermute | solution.py:305
  18.5 5.4 %collective-permute-start.11 = (bf16[528,128]{1,0:T(8,128)(2,1)S(1)}, bf16[528,128]{1,0:T(8,128)(2,1)S(1)}, u32[]{:S(2)}, u32[]{:S(2)}) collective-permute-start(bf16[528,128]{1,0:T(8,128)(2,1)S(1)} %collective-permute-done.10), channel_id=1, source_target_pairs={{2,3},{3,7},{0,11},{1,15},{6,0},{7,4},{4,8},{5,12},{10,1},{11,5},{... | collective-permute-start | bytes 405512 | tf_op jit(solution)/shard_map/ppermute | solution.py:307
  23.9 0.0 collective-permute-done.3.refs_4_
  23.9 0.0 collective-permute-done.refs_0_
  23.9 3.9 %attend.3 = (bf16[512,128]{1,0:T(8,128)(2,1)S(1)}, f32[2048,128]{1,0:T(8,128)S(1)}, bf16[2048,128]{1,0:T(8,128)(2,1)S(1)}, bf16[128,2048]{1,0:T(8,128)(2,1)S(1)}) custom-call(bf16[528,128]{1,0:T(8,128)(2,1)S(1)} %collective-permute-done.refs_0_, bf16[512,128]{1,0:T(8,128)(2,1)S(1)} %get-tuple-element.29.refs_1_, ...), custom_call_target="tpu_custom_call" | custom-call | tf_op jit(solution)/shard_map/attend/pallas_call | solution.py:323
  27.8 0.7 %collective-permute-start.4 = (bf16[512,128]{1,0:T(8,128)(2,1)S(1)}, bf16[512,128]{1,0:T(8,128)(2,1)S(1)}, u32[]{:S(2)}, u32[]{:S(2)}) collective-permute-start(bf16[512,128]{1,0:T(8,128)(2,1)S(1)} %get-tuple-element.33), channel_id=1, source_target_pairs={{0,0},{4,1},{8,2},{12,3},{1,4},{5,5},{9,6},{13,7},{2,8},{6,9},{10,... | collective-permute-start | bytes 393224 | tf_op jit(solution)/shard_map/ppermute | solution.py:354
  28.5 0.0 collective-permute-done.5.refs_0_
  28.5 0.0 collective-permute-done.7.refs_1_
  28.5 6.6 %attend.4 = (bf16[512,128]{1,0:T(8,128)(2,1)S(1)}, bf16[512,128]{1,0:T(8,128)(2,1)S(1)}, f32[2048,128]{1,0:T(8,128)S(1)}) custom-call(bf16[528,128]{1,0:T(8,128)(2,1)S(1)} %collective-permute-done.5.refs_0_, bf16[528,128]{1,0:T(8,128)(2,1)S(1)} %collective-permute-done.7.refs_1_, bf16[2048,128]{1,0:T(8,128)(2,1)S(1)} %get-tuple-element.36.refs_2_.refs_1_, ...), custom_call_target="tpu_custom_call" | custom-call | tf_op jit(solution)/shard_map/attend/pallas_call | solution.py:323
  35.2 5.1 %collective-permute-start.8 = (bf16[512,128]{1,0:T(8,128)(2,1)S(1)}, bf16[512,128]{1,0:T(8,128)(2,1)S(1)}, u32[]{:S(2)}, u32[]{:S(2)}) collective-permute-start(bf16[512,128]{1,0:T(8,128)(2,1)S(1)} %get-tuple-element.39), channel_id=1, source_target_pairs={{1,0},{5,1},{9,2},{13,3},{2,4},{6,5},{10,6},{14,7},{3,8},{7,9},{11... | collective-permute-start | bytes 393224 | tf_op jit(solution)/shard_map/ppermute | solution.py:354
  40.3 0.0 collective-permute-start.9
  40.3 0.0 collective-permute-done.11.refs_0_
  40.3 5.0 %attend.5 = (bf16[512,128]{1,0:T(8,128)(2,1)S(1)}, bf16[512,128]{1,0:T(8,128)(2,1)S(1)}, bf16[512,128]{1,0:T(8,128)(2,1)S(1)}, bf16[512,128]{1,0:T(8,128)(2,1)S(1)}, bf16[512,128]{1,0:T(8,128)(2,1)S(1)}) custom-call(bf16[528,128]{1,0:T(8,128)(2,1)S(1)} %collective-permute-done.11.refs_0_, bf16[2048,128]{1,0:T(8,128)(2,1)S(1)} %get-tuple-element.36.refs_2_.refs_1_, ...), custom_call_target="tpu_custom_call" | custom-call | tf_op jit(solution)/shard_map/attend/pallas_call | solution.py:323
  45.3 3.1 %collective-permute-start.12 = (bf16[512,128]{1,0:T(8,128)(2,1)S(1)}, bf16[512,128]{1,0:T(8,128)(2,1)S(1)}, u32[]{:S(2)}, u32[]{:S(2)}) collective-permute-start(bf16[512,128]{1,0:T(8,128)(2,1)S(1)} %get-tuple-element.43), channel_id=1, source_target_pairs={{3,0},{7,1},{11,2},{15,3},{0,4},{4,5},{8,6},{12,7},{1,8},{5,9},{9,... | collective-permute-start | bytes 393224 | tf_op jit(solution)/shard_map/ppermute | solution.py:354
  48.4 0.0 collective-permute-start.13
  48.4 0.0 collective-permute-done.4.refs_0_
  48.4 1.3 %collective-permute-start.14 = (bf16[512,128]{1,0:T(8,128)(2,1)S(1)}, bf16[512,128]{1,0:T(8,128)(2,1)S(1)}, u32[]{:S(2)}, u32[]{:S(2)}) collective-permute-start(bf16[512,128]{1,0:T(8,128)(2,1)S(1)} %get-tuple-element.48), channel_id=1, source_target_pairs={{2,0},{3,1},{0,2},{1,3},{6,4},{7,5},{4,6},{5,7},{10,8},{11,9},{8,1... | collective-permute-start | bytes 393224 | tf_op jit(solution)/shard_map/ppermute | solution.py:362
  49.6 0.0 collective-permute-done.8.refs_1_
  49.6 0.0 collective-permute-start.15
  49.6 0.0 collective-permute-done.9.refs_2_
  49.7 2.6 %collective-permute-done.12.refs_3_ = bf16[512,128]{1,0:T(8,128)(2,1)S(1)} collective-permute-done((bf16[512,128]{1,0:T(8,128)(2,1)S(1)}, bf16[512,128]{1,0:T(8,128)(2,1)S(1)}, u32[]{:S(2)}, u32[]{:S(2)}) %collective-permute-start.12) | collective-permute-done | bytes 131104 | tf_op jit(solution)/shard_map/ppermute | solution.py:354
  52.3 1.0 %unpack.2 = (bf16[512,256]{1,0:T(8,128)(2,1)}, bf16[512,256]{1,0:T(8,128)(2,1)}) custom-call(bf16[512,128]{1,0:T(8,128)(2,1)S(1)} %collective-permute-done.4.refs_0_, bf16[512,128]{1,0:T(8,128)(2,1)S(1)} %collective-permute-done.8.refs_1_, bf16[512,128]{1,0:T(8,128)(2,1)S(1)} %collective-permute-done.9.refs_2_, ...), custom_call_target="tpu_custom_call" | custom-call | tf_op jit(solution)/shard_map/unpack/pallas_call | solution.py:367
  53.3 0.0 collective-permute-done.13.refs_1_
  53.3 3.6 %collective-permute-done.14.refs_2_ = bf16[512,128]{1,0:T(8,128)(2,1)S(1)} collective-permute-done((bf16[512,128]{1,0:T(8,128)(2,1)S(1)}, bf16[512,128]{1,0:T(8,128)(2,1)S(1)}, u32[]{:S(2)}, u32[]{:S(2)}) %collective-permute-start.14) | collective-permute-done | bytes 131104 | tf_op jit(solution)/shard_map/ppermute | solution.py:362
  56.9 0.5 collective-permute-done.15.refs_3_
  57.4 1.0 %unpack.3 = (bf16[512,256]{1,0:T(8,128)(2,1)}, bf16[512,256]{1,0:T(8,128)(2,1)}) custom-call(bf16[512,128]{1,0:T(8,128)(2,1)S(1)} %get-tuple-element.46.refs_0_, bf16[512,128]{1,0:T(8,128)(2,1)S(1)} %collective-permute-done.13.refs_1_, bf16[512,128]{1,0:T(8,128)(2,1)S(1)} %collective-permute-done.14.refs_2_, bf16[512,128]{1,0:T(8,128)(2,1)S(1)} %collective-permute-done.15.refs_3_), custom_call_target="tpu_custom_call" | custom-call | tf_op jit(solution)/shard_map/unpack/pallas_call | solution.py:367
Async XLA Ops:
  2.3 8.9 %collective-permute-start.6 = (bf16[528,128]{1,0:T(8,128)(2,1)S(1)}, bf16[528,128]{1,0:T(8,128)(2,1)S(1)}, u32[]{:S(2)}, u32[]{:S(2)}) collective-permute-start(bf16[528,128]{1,0:T(8,128)(2,1)S(1)} %get-tuple-element.35), channel_id=1, source_target_pairs={{0,2},{1,3},{2,0},{3,1},{4,6},{5,7},{6,4},{7,5},{8,10},{9,11},{10,... | collective-permute-start | bytes 405512 | tf_op jit(solution)/shard_map/ppermute | solution.py:305
  5.3 5.9 %collective-permute-start.1 = (bf16[512,128]{1,0:T(8,128)(2,1)S(1)}, bf16[512,128]{1,0:T(8,128)(2,1)S(1)}, u32[]{:S(2)}, u32[]{:S(2)}) collective-permute-start(bf16[512,128]{1,0:T(8,128)(2,1)S(1)} %get-tuple-element.30), channel_id=1, source_target_pairs={{0,1},{1,2},{2,3},{3,0},{4,5},{5,6},{6,7},{7,4},{8,9},{9,10},{10,1... | collective-permute-start | bytes 393224 | tf_op jit(solution)/shard_map/ppermute | solution.py:303
  5.3 10.9 %collective-permute-start.2 = (bf16[512,128]{1,0:T(8,128)(2,1)S(1)}, bf16[512,128]{1,0:T(8,128)(2,1)S(1)}, u32[]{:S(2)}, u32[]{:S(2)}) collective-permute-start(bf16[512,128]{1,0:T(8,128)(2,1)S(1)} %get-tuple-element.31), channel_id=1, source_target_pairs={{0,2},{1,3},{2,0},{3,1},{4,6},{5,7},{6,4},{7,5},{8,10},{9,11},{10,... | collective-permute-start | bytes 393224 | tf_op jit(solution)/shard_map/ppermute | solution.py:303
  5.5 13.0 %collective-permute-start.10 = (bf16[528,128]{1,0:T(8,128)(2,1)S(1)}, bf16[528,128]{1,0:T(8,128)(2,1)S(1)}, u32[]{:S(2)}, u32[]{:S(2)}) collective-permute-start(bf16[528,128]{1,0:T(8,128)(2,1)S(1)} %get-tuple-element.41), channel_id=1, source_target_pairs={{0,2},{1,3},{2,0},{3,1},{4,6},{5,7},{6,4},{7,5},{8,10},{9,11},{10,... | collective-permute-start | bytes 405512 | tf_op jit(solution)/shard_map/ppermute | solution.py:305
  7.4 16.5 %collective-permute-start = (bf16[528,128]{1,0:T(8,128)(2,1)S(1)}, bf16[528,128]{1,0:T(8,128)(2,1)S(1)}, u32[]{:S(2)}, u32[]{:S(2)}) collective-permute-start(bf16[528,128]{1,0:T(8,128)(2,1)S(1)} %get-tuple-element.28), channel_id=1, source_target_pairs={{0,0},{1,4},{2,8},{3,12},{4,1},{5,5},{6,9},{7,13},{8,2},{9,6},{10,... | collective-permute-start | bytes 405512 | tf_op jit(solution)/shard_map/ppermute | solution.py:307
  11.2 17.3 %collective-permute-start.5 = (bf16[528,128]{1,0:T(8,128)(2,1)S(1)}, bf16[528,128]{1,0:T(8,128)(2,1)S(1)}, u32[]{:S(2)}, u32[]{:S(2)}) collective-permute-start(bf16[528,128]{1,0:T(8,128)(2,1)S(1)} %get-tuple-element.34), channel_id=1, source_target_pairs={{0,1},{1,5},{2,9},{3,13},{4,2},{5,6},{6,10},{7,14},{8,3},{9,7},{10... | collective-permute-start | bytes 405512 | tf_op jit(solution)/shard_map/ppermute | solution.py:307
  11.2 17.3 %collective-permute-start.7 = (bf16[528,128]{1,0:T(8,128)(2,1)S(1)}, bf16[528,128]{1,0:T(8,128)(2,1)S(1)}, u32[]{:S(2)}, u32[]{:S(2)}) collective-permute-start(bf16[528,128]{1,0:T(8,128)(2,1)S(1)} %collective-permute-done.6), channel_id=1, source_target_pairs={{2,2},{3,6},{0,10},{1,14},{6,3},{7,7},{4,11},{5,15},{10,0},{11,4},... | collective-permute-start | bytes 405512 | tf_op jit(solution)/shard_map/ppermute | solution.py:307
  16.2 7.6 %collective-permute-start.3 = (bf16[512,128]{1,0:T(8,128)(2,1)S(1)}, bf16[512,128]{1,0:T(8,128)(2,1)S(1)}, u32[]{:S(2)}, u32[]{:S(2)}) collective-permute-start(bf16[512,128]{1,0:T(8,128)(2,1)S(1)} %get-tuple-element.32), channel_id=1, source_target_pairs={{0,3},{1,0},{2,1},{3,2},{4,7},{5,4},{6,5},{7,6},{8,11},{9,8},{10,9... | collective-permute-start | bytes 393224 | tf_op jit(solution)/shard_map/ppermute | solution.py:303
  18.5 21.8 %collective-permute-start.11 = (bf16[528,128]{1,0:T(8,128)(2,1)S(1)}, bf16[528,128]{1,0:T(8,128)(2,1)S(1)}, u32[]{:S(2)}, u32[]{:S(2)}) collective-permute-start(bf16[528,128]{1,0:T(8,128)(2,1)S(1)} %collective-permute-done.10), channel_id=1, source_target_pairs={{2,3},{3,7},{0,11},{1,15},{6,0},{7,4},{4,8},{5,12},{10,1},{11,5},{... | collective-permute-start | bytes 405512 | tf_op jit(solution)/shard_map/ppermute | solution.py:307
  27.8 20.6 %collective-permute-start.4 = (bf16[512,128]{1,0:T(8,128)(2,1)S(1)}, bf16[512,128]{1,0:T(8,128)(2,1)S(1)}, u32[]{:S(2)}, u32[]{:S(2)}) collective-permute-start(bf16[512,128]{1,0:T(8,128)(2,1)S(1)} %get-tuple-element.33), channel_id=1, source_target_pairs={{0,0},{4,1},{8,2},{12,3},{1,4},{5,5},{9,6},{13,7},{2,8},{6,9},{10,... | collective-permute-start | bytes 393224 | tf_op jit(solution)/shard_map/ppermute | solution.py:354
  35.2 14.5 %collective-permute-start.8 = (bf16[512,128]{1,0:T(8,128)(2,1)S(1)}, bf16[512,128]{1,0:T(8,128)(2,1)S(1)}, u32[]{:S(2)}, u32[]{:S(2)}) collective-permute-start(bf16[512,128]{1,0:T(8,128)(2,1)S(1)} %get-tuple-element.39), channel_id=1, source_target_pairs={{1,0},{5,1},{9,2},{13,3},{2,4},{6,5},{10,6},{14,7},{3,8},{7,9},{11... | collective-permute-start | bytes 393224 | tf_op jit(solution)/shard_map/ppermute | solution.py:354
  40.3 9.4 %collective-permute-start.9 = (bf16[512,128]{1,0:T(8,128)(2,1)S(1)}, bf16[512,128]{1,0:T(8,128)(2,1)S(1)}, u32[]{:S(2)}, u32[]{:S(2)}) collective-permute-start(bf16[512,128]{1,0:T(8,128)(2,1)S(1)} %get-tuple-element.40), channel_id=1, source_target_pairs={{2,0},{6,1},{10,2},{14,3},{3,4},{7,5},{11,6},{15,7},{0,8},{4,9},{8... | collective-permute-start | bytes 393224 | tf_op jit(solution)/shard_map/ppermute | solution.py:354
  45.3 7.0 %collective-permute-start.12 = (bf16[512,128]{1,0:T(8,128)(2,1)S(1)}, bf16[512,128]{1,0:T(8,128)(2,1)S(1)}, u32[]{:S(2)}, u32[]{:S(2)}) collective-permute-start(bf16[512,128]{1,0:T(8,128)(2,1)S(1)} %get-tuple-element.43), channel_id=1, source_target_pairs={{3,0},{7,1},{11,2},{15,3},{0,4},{4,5},{8,6},{12,7},{1,8},{5,9},{9,... | collective-permute-start | bytes 393224 | tf_op jit(solution)/shard_map/ppermute | solution.py:354
  48.4 4.9 %collective-permute-start.13 = (bf16[512,128]{1,0:T(8,128)(2,1)S(1)}, bf16[512,128]{1,0:T(8,128)(2,1)S(1)}, u32[]{:S(2)}, u32[]{:S(2)}) collective-permute-start(bf16[512,128]{1,0:T(8,128)(2,1)S(1)} %get-tuple-element.47), channel_id=1, source_target_pairs={{1,0},{2,1},{3,2},{0,3},{5,4},{6,5},{7,6},{4,7},{9,8},{10,9},{11,1... | collective-permute-start | bytes 393224 | tf_op jit(solution)/shard_map/ppermute | solution.py:362
  48.4 8.5 %collective-permute-start.14 = (bf16[512,128]{1,0:T(8,128)(2,1)S(1)}, bf16[512,128]{1,0:T(8,128)(2,1)S(1)}, u32[]{:S(2)}, u32[]{:S(2)}) collective-permute-start(bf16[512,128]{1,0:T(8,128)(2,1)S(1)} %get-tuple-element.48), channel_id=1, source_target_pairs={{2,0},{3,1},{0,2},{1,3},{6,4},{7,5},{4,6},{5,7},{10,8},{11,9},{8,1... | collective-permute-start | bytes 393224 | tf_op jit(solution)/shard_map/ppermute | solution.py:362
  49.6 7.7 %collective-permute-start.15 = (bf16[512,128]{1,0:T(8,128)(2,1)S(1)}, bf16[512,128]{1,0:T(8,128)(2,1)S(1)}, u32[]{:S(2)}, u32[]{:S(2)}) collective-permute-start(bf16[512,128]{1,0:T(8,128)(2,1)S(1)} %get-tuple-element.49), channel_id=1, source_target_pairs={{3,0},{0,1},{1,2},{2,3},{7,4},{4,5},{5,6},{6,7},{11,8},{8,9},{9,10... | collective-permute-start | bytes 393224 | tf_op jit(solution)/shard_map/ppermute | solution.py:362
where the time goes:
time: 58 us; the launch traced here: 58.4 us
  starting transfers between devices  27.2 us (47%)
  Pallas kernels  19.2 us (33%)
  waiting for transfers between devices  11.2 us (19%)
  between operations  0.73 us (1%)
    pallas_call x3, Pallas kernels, attend(): pl.pallas_call(functools.partial(attend_body, count, chunks, first, last)...  15.5 us
    ppermute x4, starting transfers between devices, head_per_device(): lax.ppermute(hop.get(s, packed[s]), axes, [(a ^ 2, b) if s in hop else (a...  11.1 us
    ppermute x4, starting transfers between devices, head_per_device(): lax.ppermute(results[s], axes, swap(q_perm(len(ogs) + s)))  8.91 us
    ppermute x2, starting transfers between devices, head_per_device(): lax.ppermute(packed[s], 'col', [(c, c ^ 2) for c in range(chunks)])  4.92 us
    ppermute x3, waiting for transfers between devices, head_per_device(): lax.ppermute(gkv[s], 'col', swap(k_perm(s)))  4.1 us
    ppermute x3, waiting for transfers between devices, head_per_device(): lax.ppermute(packed[chunks + s], 'col', k_perm(s))  3.14 us
    ppermute x4, waiting for transfers between devices, head_per_device(): lax.ppermute(results[s], axes, swap(q_perm(len(ogs) + s)))  2.62 us
    pallas_call x2, Pallas kernels, unpack(): pl.pallas_call(functools.partial(unpack_body, axis), out_shape=[whole, wh...  2 us
  transfers between devices with their start and end apart: 16, of which 5 were waited for; matrix products, arithmetic and copies ran while one was open for 0% of the time, Pallas kernels for 28%

commit v1 on v0

--- a/solution.py
+++ b/solution.py
@@ -18,6 +18,7 @@
 NEG_FILL = -1e30
 GROUP = 2
 STREAMS = 8
+OUTS = 2
 TAIL = 16
 BATCHES = (1, 2, 1)
 HOPS = (2, 3)
@@ -94,8 +95,7 @@
     if first:
         kv_all, kv_t = take(2)
     wide, table, items, both, both_t, stat, tiles, tops, sem, table_sem = take(10)
-    (outs,) = take(1)
-    stats = take(STREAMS)
+    outs, stats = take(OUTS), take(STREAMS)
     acc = take(1)[0] if last else acc_out[0]
     scale = 1.0 / math.sqrt(HEAD)
     to_log2 = scale * math.log2(math.e)
@@ -126,7 +126,8 @@
         acc[...] = jnp.zeros_like(acc)
     else:
         acc[...] = acc_in[...]
-    outs[...] = jnp.zeros_like(outs)
+    for s in range(OUTS):
+        outs[s][...] = jnp.zeros_like(outs[s])
     for s in range(STREAMS):
         stats[s][0] = jnp.full(stats[s].shape[1:], NEG_FILL, jnp.float32)
         stats[s][1] = jnp.zeros(stats[s].shape[1:], jnp.float32)
@@ -247,15 +248,15 @@
                 acc[pl.ds(slots[u], BLK), :] += grads[u * BLK : (u + 1) * BLK]
             t = jnp.concatenate([kv_t[:, pl.ds(k, BLK)] for k in slots], axis=1)
             sums = jnp.dot(t, pair, preferred_element_type=jnp.float32)
-            outs[qb, :HEAD, :] += sums[HEAD:, BLK:]
-            outs[qb, HEAD:, :] += sums[:HEAD, :BLK]
+            outs[s % OUTS][qb, :HEAD, :] += sums[HEAD:, BLK:]
+            outs[s % OUTS][qb, HEAD:, :] += sums[:HEAD, :BLK]
         return 0
 
     lax.fori_loop(0, steps, grad_step, 0)
 
     is_out = lax.broadcasted_iota(jnp.int32, (2 * HEAD, BLK), 0) < HEAD
     for b in range(blocks):
-        out = outs[b]
+        out = functools.reduce(jnp.add, [r[b] for r in outs])
         out = jnp.where(is_out, out, out * scale)
         at = (b % per_chunk) * BLK
         og_refs[b // per_chunk][at : at + BLK, :] = out.T.astype(jnp.bfloat16)
@@ -337,7 +338,7 @@
                 pltpu.SemaphoreType.DMA((chunks,)),
                 pltpu.SemaphoreType.DMA,
             ]
-            + [pltpu.VMEM((blocks, 2 * HEAD, BLK), jnp.float32)]
+            + [pltpu.VMEM((blocks, 2 * HEAD, BLK), jnp.float32)] * OUTS
             + [pltpu.VMEM((3, blocks, BLK), jnp.float32)] * STREAMS
             + ([sums] if last else []),
             compiler_params=pltpu.CompilerParams(vmem_limit_bytes=VMEM_LIMIT),

time: 58 us -> 57.6 us (level); the launches traced: 58.4 us -> 57.1 us
  starting transfers between devices: 27.2 us -> 25.4 us
  waiting for transfers between devices: 11.2 us -> 13 us
  Pallas kernels: 19.2 us -> 18 us
    ppermute x4, starting transfers between devices: 8.91 us -> 6.46 us  [head_per_device(): lax.ppermute(results[s], axes, swap(q_perm(len(ogs) + s)))]
    pallas_call x3, Pallas kernels: 15.5 us -> 14.3 us  [attend(): pl.pallas_call(functools.partial(attend_body, count, chunks, first, last)...]
    ppermute x4, waiting for transfers between devices: 2.62 us -> 3.69 us  [head_per_device(): lax.ppermute(results[s], axes, swap(q_perm(len(ogs) + s)))]
    ppermute x3, waiting for transfers between devices: 4.1 us -> 4.82 us  [head_per_device(): lax.ppermute(gkv[s], 'col', swap(k_perm(s)))]
    ppermute x3, starting transfers between devices: 1.26 us -> 1.88 us  [head_per_device(): lax.ppermute(gkv[s], 'col', swap(k_perm(s)))]
  transfers between devices with their start and end apart: 16 -> 16, of which waited for: 5 -> 5; matrix products, arithmetic and copies ran while one was open for 0% -> 0% of each run, Pallas kernels for 28% -> 27%
where the time goes in v1:
time: 57.6 us; the launch traced here: 57.1 us
  starting transfers between devices  25.4 us (44%)
  Pallas kernels  18 us (31%)
  waiting for transfers between devices  13 us (23%)
  between operations  0.73 us (1%)
    pallas_call x3, Pallas kernels, attend(): pl.pallas_call(functools.partial(attend_body, count, chunks, first, last)...  14.3 us
    ppermute x4, starting transfers between devices, head_per_device(): lax.ppermute(hop.get(s, packed[s]), axes, [(a ^ 2, b) if s in hop else (a...  11.1 us
    ppermute x4, starting transfers between devices, head_per_device(): lax.ppermute(results[s], axes, swap(q_perm(len(ogs) + s)))  6.46 us
    ppermute x2, starting transfers between devices, head_per_device(): lax.ppermute(packed[s], 'col', [(c, c ^ 2) for c in range(chunks)])  4.92 us
    ppermute x3, waiting for transfers between devices, head_per_device(): lax.ppermute(gkv[s], 'col', swap(k_perm(s)))  4.82 us
    ppermute x4, waiting for transfers between devices, head_per_device(): lax.ppermute(results[s], axes, swap(q_perm(len(ogs) + s)))  3.69 us
    ppermute x3, waiting for transfers between devices, head_per_device(): lax.ppermute(packed[chunks + s], 'col', k_perm(s))  3.14 us
    pallas_call x2, Pallas kernels, unpack(): pl.pallas_call(functools.partial(unpack_body, axis), out_shape=[whole, wh...  2 us
  transfers between devices with their start and end apart: 16, of which 5 were waited for; matrix products, arithmetic and copies ran while one was open for 0% of the time, Pallas kernels for 27%

profile of v1, /device:TPU:0, one launch (start us, length us, event | category | flops | bytes accessed | tf_op | source)
XLA Modules:
  0.0 57.1 jit_solution(3807974060236956647)
XLA Ops:
  0.6 1.7 %pack.1 = (bf16[528,128]{1,0:T(8,128)(2,1)S(1)}, bf16[528,128]{1,0:T(8,128)(2,1)S(1)}, bf16[528,128]{1,0:T(8,128)(2,1)S(1)}, bf16[528,128]{1,0:T(8,128)(2,1)S(1)...) custom-call(s32[4,16]{1,0:T(4,128)} %lists.1, ...), custom_call_target="tpu_custom_call" | custom-call | tf_op jit(solution)/shard_map/pack/pallas_call | solution.py:281
  2.3 3.0 %collective-permute-start.6 = (bf16[528,128]{1,0:T(8,128)(2,1)S(1)}, bf16[528,128]{1,0:T(8,128)(2,1)S(1)}, u32[]{:S(2)}, u32[]{:S(2)}) collective-permute-start(bf16[528,128]{1,0:T(8,128)(2,1)S(1)} %get-tuple-element.35), channel_id=1, source_target_pairs={{0,2},{1,3},{2,0},{3,1},{4,6},{5,7},{6,4},{7,5},{8,10},{9,11},{10,... | collective-permute-start | bytes 405512 | tf_op jit(solution)/shard_map/ppermute | solution.py:306
  5.3 0.0 collective-permute-start.1
  5.3 0.1 collective-permute-start.2
  5.5 1.9 %collective-permute-start.10 = (bf16[528,128]{1,0:T(8,128)(2,1)S(1)}, bf16[528,128]{1,0:T(8,128)(2,1)S(1)}, u32[]{:S(2)}, u32[]{:S(2)}) collective-permute-start(bf16[528,128]{1,0:T(8,128)(2,1)S(1)} %get-tuple-element.41), channel_id=1, source_target_pairs={{0,2},{1,3},{2,0},{3,1},{4,6},{5,7},{6,4},{7,5},{8,10},{9,11},{10,... | collective-permute-start | bytes 405512 | tf_op jit(solution)/shard_map/ppermute | solution.py:306
  7.4 0.7 %collective-permute-start = (bf16[528,128]{1,0:T(8,128)(2,1)S(1)}, bf16[528,128]{1,0:T(8,128)(2,1)S(1)}, u32[]{:S(2)}, u32[]{:S(2)}) collective-permute-start(bf16[528,128]{1,0:T(8,128)(2,1)S(1)} %get-tuple-element.28), channel_id=1, source_target_pairs={{0,0},{1,4},{2,8},{3,12},{4,1},{5,5},{6,9},{7,13},{8,2},{9,6},{10,... | collective-permute-start | bytes 405512 | tf_op jit(solution)/shard_map/ppermute | solution.py:308
  8.0 3.1 %collective-permute-done.1.refs_2_ = bf16[512,128]{1,0:T(8,128)(2,1)S(1)} collective-permute-done((bf16[512,128]{1,0:T(8,128)(2,1)S(1)}, bf16[512,128]{1,0:T(8,128)(2,1)S(1)}, u32[]{:S(2)}, u32[]{:S(2)}) %collective-permute-start.1) | collective-permute-done | bytes 131104 | tf_op jit(solution)/shard_map/ppermute | solution.py:304
  11.2 0.0 collective-permute-start.5
  11.2 0.0 collective-permute-done.6
  11.2 5.1 %collective-permute-start.7 = (bf16[528,128]{1,0:T(8,128)(2,1)S(1)}, bf16[528,128]{1,0:T(8,128)(2,1)S(1)}, u32[]{:S(2)}, u32[]{:S(2)}) collective-permute-start(bf16[528,128]{1,0:T(8,128)(2,1)S(1)} %collective-permute-done.6), channel_id=1, source_target_pairs={{2,2},{3,6},{0,10},{1,14},{6,3},{7,7},{4,11},{5,15},{10,0},{11,4},... | collective-permute-start | bytes 405512 | tf_op jit(solution)/shard_map/ppermute | solution.py:308
  16.2 0.0 collective-permute-done.2.refs_3_
  16.2 0.9 %collective-permute-start.3 = (bf16[512,128]{1,0:T(8,128)(2,1)S(1)}, bf16[512,128]{1,0:T(8,128)(2,1)S(1)}, u32[]{:S(2)}, u32[]{:S(2)}) collective-permute-start(bf16[512,128]{1,0:T(8,128)(2,1)S(1)} %get-tuple-element.32), channel_id=1, source_target_pairs={{0,3},{1,0},{2,1},{3,2},{4,7},{5,4},{6,5},{7,6},{8,11},{9,8},{10,9... | collective-permute-start | bytes 393224 | tf_op jit(solution)/shard_map/ppermute | solution.py:304
  17.1 1.4 %collective-permute-done.10 = bf16[528,128]{1,0:T(8,128)(2,1)S(1)} collective-permute-done((bf16[528,128]{1,0:T(8,128)(2,1)S(1)}, bf16[528,128]{1,0:T(8,128)(2,1)S(1)}, u32[]{:S(2)}, u32[]{:S(2)}) %collective-permute-start.10) | collective-permute-done | bytes 135200 | tf_op jit(solution)/shard_map/ppermute | solution.py:306
  18.5 5.4 %collective-permute-start.11 = (bf16[528,128]{1,0:T(8,128)(2,1)S(1)}, bf16[528,128]{1,0:T(8,128)(2,1)S(1)}, u32[]{:S(2)}, u32[]{:S(2)}) collective-permute-start(bf16[528,128]{1,0:T(8,128)(2,1)S(1)} %collective-permute-done.10), channel_id=1, source_target_pairs={{2,3},{3,7},{0,11},{1,15},{6,0},{7,4},{4,8},{5,12},{10,1},{11,5},{... | collective-permute-start | bytes 405512 | tf_op jit(solution)/shard_map/ppermute | solution.py:308
  23.9 0.0 collective-permute-done.3.refs_4_
  23.9 0.0 collective-permute-done.refs_0_
  23.9 3.9 %attend.3 = (bf16[512,128]{1,0:T(8,128)(2,1)S(1)}, f32[2048,128]{1,0:T(8,128)S(1)}, bf16[2048,128]{1,0:T(8,128)(2,1)S(1)}, bf16[128,2048]{1,0:T(8,128)(2,1)S(1)}) custom-call(bf16[528,128]{1,0:T(8,128)(2,1)S(1)} %collective-permute-done.refs_0_, bf16[512,128]{1,0:T(8,128)(2,1)S(1)} %get-tuple-element.29.refs_1_, ...), custom_call_target="tpu_custom_call" | custom-call | tf_op jit(solution)/shard_map/attend/pallas_call | solution.py:324
  27.8 0.7 %collective-permute-start.4 = (bf16[512,128]{1,0:T(8,128)(2,1)S(1)}, bf16[512,128]{1,0:T(8,128)(2,1)S(1)}, u32[]{:S(2)}, u32[]{:S(2)}) collective-permute-start(bf16[512,128]{1,0:T(8,128)(2,1)S(1)} %get-tuple-element.33), channel_id=1, source_target_pairs={{0,0},{4,1},{8,2},{12,3},{1,4},{5,5},{9,6},{13,7},{2,8},{6,9},{10,... | collective-permute-start | bytes 393224 | tf_op jit(solution)/shard_map/ppermute | solution.py:355
  28.5 0.0 collective-permute-done.5.refs_0_
  28.5 0.0 collective-permute-done.7.refs_1_
  28.5 6.7 %attend.4 = (bf16[512,128]{1,0:T(8,128)(2,1)S(1)}, bf16[512,128]{1,0:T(8,128)(2,1)S(1)}, f32[2048,128]{1,0:T(8,128)S(1)}) custom-call(bf16[528,128]{1,0:T(8,128)(2,1)S(1)} %collective-permute-done.5.refs_0_, bf16[528,128]{1,0:T(8,128)(2,1)S(1)} %collective-permute-done.7.refs_1_, bf16[2048,128]{1,0:T(8,128)(2,1)S(1)} %get-tuple-element.36.refs_2_.refs_1_, ...), custom_call_target="tpu_custom_call" | custom-call | tf_op jit(solution)/shard_map/attend/pallas_call | solution.py:324
  35.2 3.9 %collective-permute-start.8 = (bf16[512,128]{1,0:T(8,128)(2,1)S(1)}, bf16[512,128]{1,0:T(8,128)(2,1)S(1)}, u32[]{:S(2)}, u32[]{:S(2)}) collective-permute-start(bf16[512,128]{1,0:T(8,128)(2,1)S(1)} %get-tuple-element.39), channel_id=1, source_target_pairs={{1,0},{5,1},{9,2},{13,3},{2,4},{6,5},{10,6},{14,7},{3,8},{7,9},{11... | collective-permute-start | bytes 393224 | tf_op jit(solution)/shard_map/ppermute | solution.py:355
  39.1 1.9 %collective-permute-start.9 = (bf16[512,128]{1,0:T(8,128)(2,1)S(1)}, bf16[512,128]{1,0:T(8,128)(2,1)S(1)}, u32[]{:S(2)}, u32[]{:S(2)}) collective-permute-start(bf16[512,128]{1,0:T(8,128)(2,1)S(1)} %get-tuple-element.40), channel_id=1, source_target_pairs={{2,0},{6,1},{10,2},{14,3},{3,4},{7,5},{11,6},{15,7},{0,8},{4,9},{8... | collective-permute-start | bytes 393224 | tf_op jit(solution)/shard_map/ppermute | solution.py:355
  40.9 0.0 collective-permute-done.11.refs_0_
  40.9 3.7 %attend.5 = (bf16[512,128]{1,0:T(8,128)(2,1)S(1)}, bf16[512,128]{1,0:T(8,128)(2,1)S(1)}, bf16[512,128]{1,0:T(8,128)(2,1)S(1)}, bf16[512,128]{1,0:T(8,128)(2,1)S(1)}, bf16[512,128]{1,0:T(8,128)(2,1)S(1)}) custom-call(bf16[528,128]{1,0:T(8,128)(2,1)S(1)} %collective-permute-done.11.refs_0_, bf16[2048,128]{1,0:T(8,128)(2,1)S(1)} %get-tuple-element.36.refs_2_.refs_1_, ...), custom_call_target="tpu_custom_call" | custom-call | tf_op jit(solution)/shard_map/attend/pallas_call | solution.py:324
  44.6 0.1 collective-permute-start.12
  44.7 1.7 %collective-permute-start.13 = (bf16[512,128]{1,0:T(8,128)(2,1)S(1)}, bf16[512,128]{1,0:T(8,128)(2,1)S(1)}, u32[]{:S(2)}, u32[]{:S(2)}) collective-permute-start(bf16[512,128]{1,0:T(8,128)(2,1)S(1)} %get-tuple-element.47), channel_id=1, source_target_pairs={{1,0},{2,1},{3,2},{0,3},{5,4},{6,5},{7,6},{4,7},{9,8},{10,9},{11,1... | collective-permute-start | bytes 393224 | tf_op jit(solution)/shard_map/ppermute | solution.py:363
  46.4 0.0 collective-permute-done.4.refs_0_
  46.4 0.0 collective-permute-start.14
  46.5 0.0 collective-permute-done.8.refs_1_
  46.5 0.1 collective-permute-start.15
  46.6 0.0 collective-permute-done.9.refs_2_
  46.6 3.7 %collective-permute-done.12.refs_3_ = bf16[512,128]{1,0:T(8,128)(2,1)S(1)} collective-permute-done((bf16[512,128]{1,0:T(8,128)(2,1)S(1)}, bf16[512,128]{1,0:T(8,128)(2,1)S(1)}, u32[]{:S(2)}, u32[]{:S(2)}) %collective-permute-start.12) | collective-permute-done | bytes 131104 | tf_op jit(solution)/shard_map/ppermute | solution.py:355
  50.3 1.0 %unpack.2 = (bf16[512,256]{1,0:T(8,128)(2,1)}, bf16[512,256]{1,0:T(8,128)(2,1)}) custom-call(bf16[512,128]{1,0:T(8,128)(2,1)S(1)} %collective-permute-done.4.refs_0_, bf16[512,128]{1,0:T(8,128)(2,1)S(1)} %collective-permute-done.8.refs_1_, bf16[512,128]{1,0:T(8,128)(2,1)S(1)} %collective-permute-done.9.refs_2_, ...), custom_call_target="tpu_custom_call" | custom-call | tf_op jit(solution)/shard_map/unpack/pallas_call | solution.py:368
  51.3 0.0 collective-permute-done.13.refs_1_
  51.3 3.7 %collective-permute-done.14.refs_2_ = bf16[512,128]{1,0:T(8,128)(2,1)S(1)} collective-permute-done((bf16[512,128]{1,0:T(8,128)(2,1)S(1)}, bf16[512,128]{1,0:T(8,128)(2,1)S(1)}, u32[]{:S(2)}, u32[]{:S(2)}) %collective-permute-start.14) | collective-permute-done | bytes 131104 | tf_op jit(solution)/shard_map/ppermute | solution.py:363
  55.0 1.1 %collective-permute-done.15.refs_3_ = bf16[512,128]{1,0:T(8,128)(2,1)S(1)} collective-permute-done((bf16[512,128]{1,0:T(8,128)(2,1)S(1)}, bf16[512,128]{1,0:T(8,128)(2,1)S(1)}, u32[]{:S(2)}, u32[]{:S(2)}) %collective-permute-start.15) | collective-permute-done | bytes 131104 | tf_op jit(solution)/shard_map/ppermute | solution.py:363
  56.1 1.0 %unpack.3 = (bf16[512,256]{1,0:T(8,128)(2,1)}, bf16[512,256]{1,0:T(8,128)(2,1)}) custom-call(bf16[512,128]{1,0:T(8,128)(2,1)S(1)} %get-tuple-element.46.refs_0_, bf16[512,128]{1,0:T(8,128)(2,1)S(1)} %collective-permute-done.13.refs_1_, bf16[512,128]{1,0:T(8,128)(2,1)S(1)} %collective-permute-done.14.refs_2_, bf16[512,128]{1,0:T(8,128)(2,1)S(1)} %collective-permute-done.15.refs_3_), custom_call_target="tpu_custom_call" | custom-call | tf_op jit(solution)/shard_map/unpack/pallas_call | solution.py:368
Async XLA Ops:
  2.3 8.9 %collective-permute-start.6 = (bf16[528,128]{1,0:T(8,128)(2,1)S(1)}, bf16[528,128]{1,0:T(8,128)(2,1)S(1)}, u32[]{:S(2)}, u32[]{:S(2)}) collective-permute-start(bf16[528,128]{1,0:T(8,128)(2,1)S(1)} %get-tuple-element.35), channel_id=1, source_target_pairs={{0,2},{1,3},{2,0},{3,1},{4,6},{5,7},{6,4},{7,5},{8,10},{9,11},{10,... | collective-permute-start | bytes 405512 | tf_op jit(solution)/shard_map/ppermute | solution.py:306
  5.3 5.9 %collective-permute-start.1 = (bf16[512,128]{1,0:T(8,128)(2,1)S(1)}, bf16[512,128]{1,0:T(8,128)(2,1)S(1)}, u32[]{:S(2)}, u32[]{:S(2)}) collective-permute-start(bf16[512,128]{1,0:T(8,128)(2,1)S(1)} %get-tuple-element.30), channel_id=1, source_target_pairs={{0,1},{1,2},{2,3},{3,0},{4,5},{5,6},{6,7},{7,4},{8,9},{9,10},{10,1... | collective-permute-start | bytes 393224 | tf_op jit(solution)/shard_map/ppermute | solution.py:304
  5.3 10.9 %collective-permute-start.2 = (bf16[512,128]{1,0:T(8,128)(2,1)S(1)}, bf16[512,128]{1,0:T(8,128)(2,1)S(1)}, u32[]{:S(2)}, u32[]{:S(2)}) collective-permute-start(bf16[512,128]{1,0:T(8,128)(2,1)S(1)} %get-tuple-element.31), channel_id=1, source_target_pairs={{0,2},{1,3},{2,0},{3,1},{4,6},{5,7},{6,4},{7,5},{8,10},{9,11},{10,... | collective-permute-start | bytes 393224 | tf_op jit(solution)/shard_map/ppermute | solution.py:304
  5.5 13.0 %collective-permute-start.10 = (bf16[528,128]{1,0:T(8,128)(2,1)S(1)}, bf16[528,128]{1,0:T(8,128)(2,1)S(1)}, u32[]{:S(2)}, u32[]{:S(2)}) collective-permute-start(bf16[528,128]{1,0:T(8,128)(2,1)S(1)} %get-tuple-element.41), channel_id=1, source_target_pairs={{0,2},{1,3},{2,0},{3,1},{4,6},{5,7},{6,4},{7,5},{8,10},{9,11},{10,... | collective-permute-start | bytes 405512 | tf_op jit(solution)/shard_map/ppermute | solution.py:306
  7.4 16.5 %collective-permute-start = (bf16[528,128]{1,0:T(8,128)(2,1)S(1)}, bf16[528,128]{1,0:T(8,128)(2,1)S(1)}, u32[]{:S(2)}, u32[]{:S(2)}) collective-permute-start(bf16[528,128]{1,0:T(8,128)(2,1)S(1)} %get-tuple-element.28), channel_id=1, source_target_pairs={{0,0},{1,4},{2,8},{3,12},{4,1},{5,5},{6,9},{7,13},{8,2},{9,6},{10,... | collective-permute-start | bytes 405512 | tf_op jit(solution)/shard_map/ppermute | solution.py:308
  11.2 17.3 %collective-permute-start.5 = (bf16[528,128]{1,0:T(8,128)(2,1)S(1)}, bf16[528,128]{1,0:T(8,128)(2,1)S(1)}, u32[]{:S(2)}, u32[]{:S(2)}) collective-permute-start(bf16[528,128]{1,0:T(8,128)(2,1)S(1)} %get-tuple-element.34), channel_id=1, source_target_pairs={{0,1},{1,5},{2,9},{3,13},{4,2},{5,6},{6,10},{7,14},{8,3},{9,7},{10... | collective-permute-start | bytes 405512 | tf_op jit(solution)/shard_map/ppermute | solution.py:308
  11.2 17.3 %collective-permute-start.7 = (bf16[528,128]{1,0:T(8,128)(2,1)S(1)}, bf16[528,128]{1,0:T(8,128)(2,1)S(1)}, u32[]{:S(2)}, u32[]{:S(2)}) collective-permute-start(bf16[528,128]{1,0:T(8,128)(2,1)S(1)} %collective-permute-done.6), channel_id=1, source_target_pairs={{2,2},{3,6},{0,10},{1,14},{6,3},{7,7},{4,11},{5,15},{10,0},{11,4},... | collective-permute-start | bytes 405512 | tf_op jit(solution)/shard_map/ppermute | solution.py:308
  16.2 7.6 %collective-permute-start.3 = (bf16[512,128]{1,0:T(8,128)(2,1)S(1)}, bf16[512,128]{1,0:T(8,128)(2,1)S(1)}, u32[]{:S(2)}, u32[]{:S(2)}) collective-permute-start(bf16[512,128]{1,0:T(8,128)(2,1)S(1)} %get-tuple-element.32), channel_id=1, source_target_pairs={{0,3},{1,0},{2,1},{3,2},{4,7},{5,4},{6,5},{7,6},{8,11},{9,8},{10,9... | collective-permute-start | bytes 393224 | tf_op jit(solution)/shard_map/ppermute | solution.py:304
  18.5 22.4 %collective-permute-start.11 = (bf16[528,128]{1,0:T(8,128)(2,1)S(1)}, bf16[528,128]{1,0:T(8,128)(2,1)S(1)}, u32[]{:S(2)}, u32[]{:S(2)}) collective-permute-start(bf16[528,128]{1,0:T(8,128)(2,1)S(1)} %collective-permute-done.10), channel_id=1, source_target_pairs={{2,3},{3,7},{0,11},{1,15},{6,0},{7,4},{4,8},{5,12},{10,1},{11,5},{... | collective-permute-start | bytes 405512 | tf_op jit(solution)/shard_map/ppermute | solution.py:308
  27.8 18.7 %collective-permute-start.4 = (bf16[512,128]{1,0:T(8,128)(2,1)S(1)}, bf16[512,128]{1,0:T(8,128)(2,1)S(1)}, u32[]{:S(2)}, u32[]{:S(2)}) collective-permute-start(bf16[512,128]{1,0:T(8,128)(2,1)S(1)} %get-tuple-element.33), channel_id=1, source_target_pairs={{0,0},{4,1},{8,2},{12,3},{1,4},{5,5},{9,6},{13,7},{2,8},{6,9},{10,... | collective-permute-start | bytes 393224 | tf_op jit(solution)/shard_map/ppermute | solution.py:355
  35.2 11.3 %collective-permute-start.8 = (bf16[512,128]{1,0:T(8,128)(2,1)S(1)}, bf16[512,128]{1,0:T(8,128)(2,1)S(1)}, u32[]{:S(2)}, u32[]{:S(2)}) collective-permute-start(bf16[512,128]{1,0:T(8,128)(2,1)S(1)} %get-tuple-element.39), channel_id=1, source_target_pairs={{1,0},{5,1},{9,2},{13,3},{2,4},{6,5},{10,6},{14,7},{3,8},{7,9},{11... | collective-permute-start | bytes 393224 | tf_op jit(solution)/shard_map/ppermute | solution.py:355
  39.1 7.5 %collective-permute-start.9 = (bf16[512,128]{1,0:T(8,128)(2,1)S(1)}, bf16[512,128]{1,0:T(8,128)(2,1)S(1)}, u32[]{:S(2)}, u32[]{:S(2)}) collective-permute-start(bf16[512,128]{1,0:T(8,128)(2,1)S(1)} %get-tuple-element.40), channel_id=1, source_target_pairs={{2,0},{6,1},{10,2},{14,3},{3,4},{7,5},{11,6},{15,7},{0,8},{4,9},{8... | collective-permute-start | bytes 393224 | tf_op jit(solution)/shard_map/ppermute | solution.py:355
  44.6 5.7 %collective-permute-start.12 = (bf16[512,128]{1,0:T(8,128)(2,1)S(1)}, bf16[512,128]{1,0:T(8,128)(2,1)S(1)}, u32[]{:S(2)}, u32[]{:S(2)}) collective-permute-start(bf16[512,128]{1,0:T(8,128)(2,1)S(1)} %get-tuple-element.43), channel_id=1, source_target_pairs={{3,0},{7,1},{11,2},{15,3},{0,4},{4,5},{8,6},{12,7},{1,8},{5,9},{9,... | collective-permute-start | bytes 393224 | tf_op jit(solution)/shard_map/ppermute | solution.py:355
  44.7 6.6 %collective-permute-start.13 = (bf16[512,128]{1,0:T(8,128)(2,1)S(1)}, bf16[512,128]{1,0:T(8,128)(2,1)S(1)}, u32[]{:S(2)}, u32[]{:S(2)}) collective-permute-start(bf16[512,128]{1,0:T(8,128)(2,1)S(1)} %get-tuple-element.47), channel_id=1, source_target_pairs={{1,0},{2,1},{3,2},{0,3},{5,4},{6,5},{7,6},{4,7},{9,8},{10,9},{11,1... | collective-permute-start | bytes 393224 | tf_op jit(solution)/shard_map/ppermute | solution.py:363
  46.4 8.6 %collective-permute-start.14 = (bf16[512,128]{1,0:T(8,128)(2,1)S(1)}, bf16[512,128]{1,0:T(8,128)(2,1)S(1)}, u32[]{:S(2)}, u32[]{:S(2)}) collective-permute-start(bf16[512,128]{1,0:T(8,128)(2,1)S(1)} %get-tuple-element.48), channel_id=1, source_target_pairs={{2,0},{3,1},{0,2},{1,3},{6,4},{7,5},{4,6},{5,7},{10,8},{11,9},{8,1... | collective-permute-start | bytes 393224 | tf_op jit(solution)/shard_map/ppermute | solution.py:363
  46.5 9.6 %collective-permute-start.15 = (bf16[512,128]{1,0:T(8,128)(2,1)S(1)}, bf16[512,128]{1,0:T(8,128)(2,1)S(1)}, u32[]{:S(2)}, u32[]{:S(2)}) collective-permute-start(bf16[512,128]{1,0:T(8,128)(2,1)S(1)} %get-tuple-element.49), channel_id=1, source_target_pairs={{3,0},{0,1},{1,2},{2,3},{7,4},{4,5},{5,6},{6,7},{11,8},{8,9},{9,10... | collective-permute-start | bytes 393224 | tf_op jit(solution)/shard_map/ppermute | solution.py:363
